TPU v7x, 256 devices: a whole 4x4x8 slice. The times are simulated.
256 devices in a mesh: grp: 32 (over x, y, core), blk: 8 (over z).
Axes of the slice: x: 4, y: 4, z: 8, core: 2. Of those that a mesh axis runs over, the one named last changes fastest.
Arguments:
- tiles_near: bfloat16 [16384, 256, 256], P(('grp', 'blk')), may hold values from -0.078125 to 0.078125
- near_cols: int32 [256, 64], P(('grp', 'blk')), may hold values from 0 to 3
- tiles_far: bfloat16 [6144, 256, 256], P(('grp', 'blk')), may hold values from -0.078125 to 0.078125
- far_groups: int32 [256, 24], P(('grp', 'blk')), may hold values from 0 to 31, as said below
- need_blocks: int32 [256, 32], P(('grp', 'blk')), may hold values from -1 to 3, as said below
- start_vectors: bfloat16 [262144, 128], P(('grp', 'blk')), may hold values from -6 to 6
Outputs:
- vectors: float32 [262144, 128], P(('grp', 'blk'))
Inputs may be any that keep to these rules, and one draw needn't show every extreme that they name: need_blocks[d, h] is -1 for d's own group and for groups d reads nothing from, else a row block index below 4 of the device of group h at d's position along blk; every device reads from at least one other group. far_groups[d, t] is a group h with need_blocks[d, h] >= 0.
All inputs are finite; a program needn't handle non-finite values.
Results may differ from a plain program's by a relative error of at most 0.0029.
Values may be sent and summed in bfloat16 or wider, within the bound.
A program may use at most 128 MiB of HBM per device.

v0:
```python
import jax
import jax.numpy as jnp
from jax import lax
from jax.sharding import PartitionSpec as P

ITERS = 2


def per_device(tiles_near, near_cols, tiles_far, far_groups, need_blocks, start_vectors):
    tile_size = tiles_near.shape[1]
    vec_width = start_vectors.shape[1]
    blocks = start_vectors.shape[0] // tile_size
    group_size = lax.axis_size("blk")
    group_count = lax.axis_size("grp")
    per_source = tiles_near.shape[0] // (blocks * group_size)
    far_each = tiles_far.shape[0] // blocks
    near_tiles = tiles_near.reshape(blocks, group_size, per_source, tile_size, tile_size)
    near_index = near_cols.reshape(blocks, group_size, per_source)
    far_tiles = tiles_far.reshape(blocks, far_each, tile_size, tile_size)
    far_index = far_groups.reshape(blocks, far_each)
    wanted = need_blocks.reshape(group_count)
    total_rows = blocks * tile_size * group_size * group_count
    current = start_vectors
    vectors = start_vectors.astype(jnp.float32)
    for iteration in range(ITERS):
        local_rows = current.reshape(blocks, tile_size, vec_width)
        group_table = lax.all_gather(local_rows, "blk", axis=0, tiled=True)
        source_ids = jnp.arange(group_size, dtype=jnp.int32)[None, :, None]
        chosen = group_table[source_ids * blocks + near_index]
        near_part = jnp.einsum(
            "rmnij,rmnjk->rik", near_tiles, chosen, preferred_element_type=jnp.float32
        )
        everything = lax.all_gather(local_rows, "grp", axis=0, tiled=True)
        far_rows = everything[far_index * blocks + wanted[far_index]]
        far_part = jnp.einsum(
            "rnij,rnjk->rik", far_tiles, far_rows, preferred_element_type=jnp.float32
        )
        product = near_part + far_part
        flat_rows = product.reshape(blocks * tile_size, vec_width)
        local_gram = jnp.dot(
            flat_rows.T,
            flat_rows,
            precision=lax.Precision.HIGHEST,
            preferred_element_type=jnp.float32,
        )
        gram = lax.psum(local_gram, ("grp", "blk")) / total_rows
        factor = jnp.linalg.cholesky(gram)
        identity_matrix = jnp.eye(vec_width, dtype=jnp.float32)
        inverse = lax.linalg.triangular_solve(factor, identity_matrix, left_side=True, lower=True).T
        vectors = jnp.dot(
            flat_rows, inverse, precision=lax.Precision.HIGHEST, preferred_element_type=jnp.float32
        )
        current = vectors.astype(jnp.bfloat16)
    return vectors


def solution(mesh):
    in_specs = (
        P(("grp", "blk"), None, None),
        P(("grp", "blk"), None),
        P(("grp", "blk"), None, None),
        P(("grp", "blk"), None),
        P(("grp", "blk"), None),
        P(("grp", "blk"), None),
    )
    out_specs = P(("grp", "blk"), None)
    return jax.shard_map(
        per_device, mesh=mesh, in_specs=in_specs, out_specs=out_specs, check_vma=False
    )
```

profile of v0, /device:TPU:1, one launch (start us, length us, event | category | flops | bytes accessed | tf_op | source)
XLA Modules:
  0.0 777.3 jit_solution(7489281376360508679)
XLA Ops:
  10.1 1.4 gather_fusion.1
  11.6 1.3 reduce.11
  13.3 37.1 %all-gather.5.cloned.1.call-done = bf16[32,256,128]{2,1,0:T(8,128)(2,1)} async-done(((bf16[4,256,128]{2,1,0:T(8,128)(2,1)}), bf16[32,256,128]{2,1,0:T(8,128)(2,1)}) %all-gather.5.cloned.1.call-update) | async-done | bytes 2097168 | tf_op jit(solution)/shard_map/all_gather | solution.py:27
  50.4 4.6 gather_fusion
  55.0 58.5 %all-gather.7.cloned.1.call-done = bf16[128,256,128]{2,1,0:T(8,128)(2,1)} async-done(((bf16[4,256,128]{2,1,0:T(8,128)(2,1)}), bf16[128,256,128]{2,1,0:T(8,128)(2,1)}) %all-gather.7.cloned.1.call-update) | async-done | bytes 8388624 | tf_op jit(solution)/shard_map/all_gather | solution.py:33
  113.6 5.4 gather_fusion.2
  118.9 2.7 convolution_bitcast_fusion.1
  121.7 5.2 fusion.31
  129.0 2.0 copy.32
  131.0 235.3 %all-reduce.3.cloned.1.call-done = f32[128,128]{0,1:T(8,128)} async-done(((f32[128,128]{0,1:T(8,128)}), f32[128,128]{0,1:T(8,128)}) %all-reduce.3.cloned.1.call-update) | async-done | bytes 65552 | tf_op jit(solution)/shard_map/psum | solution.py:46
  368.1 11.7 %cholesky.44 = f32[128,128]{1,0:T(8,128)S(1)} custom-call(f32[128,128]{1,0:T(8,128)S(1)} %fusion.45), custom_call_target="Cholesky" | custom-call | tf_op jit(solution)/shard_map/jit(cholesky)/cholesky | solution.py:47
  381.2 9.8 %custom-call.6 = f32[1,128,128]{1,2,0:T(8,128)S(1)} custom-call(f32[1,128,128]{2,1,0:T(8,128)S(1)} %fusion.40), custom_call_target="InvertDiagBlocksLowerTriangular" | custom-call | tf_op jit(solution)/shard_map/triangular_solve/custom-call.0 | solution.py:49
  391.3 2.3 convolution_convert_fusion
  394.5 32.8 %all-gather.9.cloned.1.call-done = bf16[32,256,128]{2,1,0:T(8,128)(2,1)} async-done(((bf16[4,256,128]{2,1,0:T(8,128)(2,1)}), bf16[32,256,128]{2,1,0:T(8,128)(2,1)}) %all-gather.9.cloned.1.call-update) | async-done | bytes 2097168 | tf_op jit(solution)/shard_map/all_gather | solution.py:27
  427.3 4.6 gather_fusion.3
  432.0 58.4 %all-gather.11.cloned.1.call-done = bf16[128,256,128]{2,1,0:T(8,128)(2,1)} async-done(((bf16[4,256,128]{2,1,0:T(8,128)(2,1)}), bf16[128,256,128]{2,1,0:T(8,128)(2,1)}) %all-gather.11.cloned.1.call-update) | async-done | bytes 8388624 | tf_op jit(solution)/shard_map/all_gather | solution.py:33
  490.3 5.4 gather_fusion.4
  495.7 2.7 convolution_bitcast_fusion
  498.4 5.2 fusion.21
  505.7 2.0 copy.39
  507.7 235.3 %all-reduce.5.cloned.1.call-done = f32[128,128]{0,1:T(8,128)} async-done(((f32[128,128]{0,1:T(8,128)}), f32[128,128]{0,1:T(8,128)}) %all-reduce.5.cloned.1.call-update) | async-done | bytes 65552 | tf_op jit(solution)/shard_map/psum | solution.py:46
  744.9 11.7 %cholesky.55 = f32[128,128]{1,0:T(8,128)S(1)} custom-call(f32[128,128]{1,0:T(8,128)S(1)} %fusion.43), custom_call_target="Cholesky" | custom-call | tf_op jit(solution)/shard_map/jit(cholesky)/cholesky | solution.py:47
  757.9 9.8 %custom-call.7 = f32[1,128,128]{1,2,0:T(8,128)S(1)} custom-call(f32[1,128,128]{2,1,0:T(8,128)S(1)} %fusion.41), custom_call_target="InvertDiagBlocksLowerTriangular" | custom-call | tf_op jit(solution)/shard_map/triangular_solve/custom-call.0 | solution.py:49
  768.0 2.4 fusion.46
  (53 shorter events, 15.7 us)
Async XLA Ops:
  6.5 112.4 %copy-start = (bf16[24,256,256]{2,1,0:T(8,128)(2,1)S(1)}, bf16[24,256,256]{2,1,0:T(8,128)(2,1)}, u32[]{:S(2)}) copy-start(bf16[24,256,256]{2,1,0:T(8,128)(2,1)} %param.11) | copy-start | bytes 9437188
  6.5 43.8 %all-gather.5.cloned.1.call-start = ((), (), s32[]{:S(2)}) async-start(), calls=%async_computation | async-start | bytes 2359296 | tf_op jit(solution)/shard_map/all_gather | solution.py:27
  7.3 106.3 %all-gather.7.cloned.1.call-start = ((), (), s32[]{:S(2)}) async-start(), calls=%async_computation.1 | async-start | bytes 8650752 | tf_op jit(solution)/shard_map/all_gather | solution.py:33
  8.0 358.3 %all-reduce.3.cloned.1.call-start = ((), (), s32[]{:S(2)}) async-start(), calls=%async_computation.2 | async-start | bytes 131072 | tf_op jit(solution)/shard_map/psum | solution.py:46
  118.9 2.7 copy-start.4
  126.9 0.8 copy-start.1
  128.9 298.4 %all-gather.9.cloned.1.call-start = ((), (), s32[]{:S(2)}) async-start(), calls=%async_computation.3 | async-start | bytes 2359296 | tf_op jit(solution)/shard_map/all_gather | solution.py:27
  393.6 96.7 %all-gather.11.cloned.1.call-start = ((), (), s32[]{:S(2)}) async-start(), calls=%async_computation.4 | async-start | bytes 8650752 | tf_op jit(solution)/shard_map/all_gather | solution.py:33
  394.2 348.8 %all-reduce.5.cloned.1.call-start = ((), (), s32[]{:S(2)}) async-start(), calls=%async_computation.5 | async-start | bytes 131072 | tf_op jit(solution)/shard_map/psum | solution.py:46
  495.7 2.7 copy-start.3
  503.7 0.8 copy-start.2
Sparse Core Ops, SparseCore 0:
  9.1 41.1 all-gather.4
  52.9 60.5 all-gather.6
  129.1 237.2 all-reduce.2
  393.8 33.4 all-gather.8
  429.7 60.5 all-gather.10
  505.8 237.1 all-reduce.4
where the time goes:
time: 778 us; the launch traced here: 777 us
  waiting for transfers between devices  659 us (85%)
  other arithmetic  51.9 us (7%)
  local copies, waits for them, and re-layouts  28.3 us (4%)
  matrix products  23.6 us (3%)
  between operations  13.7 us (2%)
    psum x2, waiting for transfers between devices, per_device(): gram = lax.psum(local_gram, ('grp', 'blk')) / total_rows  471 us
    all_gather x2, waiting for transfers between devices, per_device(): everything = lax.all_gather(local_rows, 'grp', axis=0, tiled=True)  117 us
    all_gather x2, waiting for transfers between devices, per_device(): group_table = lax.all_gather(local_rows, 'blk', axis=0, tiled=True)  70 us
    another operation x6, other arithmetic, per_device(): factor = jnp.linalg.cholesky(gram)  24.8 us
    another operation x4, other arithmetic, per_device(): lax.linalg.triangular_solve(factor, identity_matrix, left_side=True, lowe...  20.9 us
  transfers between devices with their start and end apart: 6, of which 6 were waited for; matrix products, arithmetic and copies ran while one was open for 2% of the time, Pallas kernels for 0%

commit v1 on v0

--- a/solution.py
+++ b/solution.py
@@ -24,7 +24,9 @@
     vectors = start_vectors.astype(jnp.float32)
     for iteration in range(ITERS):
         local_rows = current.reshape(blocks, tile_size, vec_width)
-        group_table = lax.all_gather(local_rows, "blk", axis=0, tiled=True)
+        group_table = jnp.concatenate(
+            lax.all_to_all(jnp.stack([local_rows] * lax.axis_size("blk")), "blk", 0, 0), axis=0
+        )
         source_ids = jnp.arange(group_size, dtype=jnp.int32)[None, :, None]
         chosen = group_table[source_ids * blocks + near_index]
         near_part = jnp.einsum(

time: 778 us -> 697 us (0.90)
  waiting for transfers between devices: 659 us -> 513 us
  blocking collectives: 0 us -> 54.4 us
  starting transfers between devices: 0.38 us -> 9.17 us
    all_gather x2, waiting for transfers between devices: 117 us -> 0.01 us  [per_device(): everything = lax.all_gather(local_rows, 'grp', axis=0, tiled=True)]
    all_gather x2 -> x0, waiting for transfers between devices: 70 us -> none  [per_device(): group_table = lax.all_gather(local_rows, 'blk', axis=0, tiled=True)]
    all_to_all x0 -> x1, blocking collectives: none -> 54.4 us  [per_device(): lax.all_to_all(jnp.stack([local_rows] * lax.axis_size('blk')), 'blk', 0, 0)]
    all_to_all x0 -> x1, waiting for transfers between devices: none -> 45.2 us  [per_device(): lax.all_to_all(jnp.stack([local_rows] * lax.axis_size('blk')), 'blk', 0, 0)]
    all_to_all x0 -> x1, starting transfers between devices: none -> 9.01 us  [per_device(): lax.all_to_all(jnp.stack([local_rows] * lax.axis_size('blk')), 'blk', 0, 0)]
  transfers between devices with their start and end apart: 6 -> 5, of which waited for: 6 -> 3; matrix products, arithmetic and copies ran while one was open for 2% -> 3% of each run, Pallas kernels for 0% -> 0%
where the time goes in v1:
time: 697 us; the launch traced here: 696 us
  waiting for transfers between devices  513 us (74%)
  blocking collectives  54.4 us (8%)
  other arithmetic  50.6 us (7%)
  local copies, waits for them, and re-layouts  32 us (5%)
  matrix products  23.6 us (3%)
  between operations  13.3 us (2%)
  starting transfers between devices  9.17 us (1%)
    psum x2, waiting for transfers between devices, per_device(): gram = lax.psum(local_gram, ('grp', 'blk')) / total_rows  467 us
    all_to_all x1, blocking collectives, per_device(): lax.all_to_all(jnp.stack([local_rows] * lax.axis_size('blk')), 'blk', 0, 0)  54.4 us
    all_to_all x1, waiting for transfers between devices, per_device(): lax.all_to_all(jnp.stack([local_rows] * lax.axis_size('blk')), 'blk', 0, 0)  45.2 us
    another operation x6, other arithmetic, per_device(): factor = jnp.linalg.cholesky(gram)  24.8 us
    another operation x4, other arithmetic, per_device(): lax.linalg.triangular_solve(factor, identity_matrix, left_side=True, lowe...  20.9 us
  transfers between devices with their start and end apart: 5, of which 3 were waited for; matrix products, arithmetic and copies ran while one was open for 3% of the time, Pallas kernels for 0%

profile of v1, /device:TPU:1, one launch (start us, length us, event | category | flops | bytes accessed | tf_op | source)
XLA Modules:
  0.0 695.9 jit_solution(209102806035530164)
XLA Ops:
  7.3 3.0 stack.6
  10.2 9.0 %all-to-all-start = ((bf16[8,4,256,128]{3,2,1,0:T(8,128)(2,1)}), bf16[8,4,256,128]{3,2,1,0:T(8,128)(2,1)}, u32[]{:S(2)}, u32[]{:S(2)}) async-start(bf16[8,4,256,128]{3,2,1,0:T(8,128)(2,1)} %stack.6), calls=%async_computation | async-start | bytes 4194304 | tf_op jit(solution)/shard_map/all_to_all | solution.py:28
  22.6 45.2 %all-to-all-done = bf16[8,4,256,128]{3,2,1,0:T(8,128)(2,1)} async-done(((bf16[8,4,256,128]{3,2,1,0:T(8,128)(2,1)}), bf16[8,4,256,128]{3,2,1,0:T(8,128)(2,1)}, u32[]{:S(2)}, u32[]{:S(2)}) %all-to-all-start) | async-done | bytes 2097184 | tf_op jit(solution)/shard_map/all_to_all | solution.py:28
  67.8 4.6 gather_fusion
  72.4 5.4 gather_fusion.2
  77.8 2.7 convolution_bitcast_fusion.1
  80.6 5.2 fusion.31
  86.6 1.2 convolution_bitcast_fusion.3
  87.9 2.0 copy.30
  89.9 235.6 %all-reduce.3.cloned.1.call-done = f32[128,128]{0,1:T(8,128)} async-done(((f32[128,128]{0,1:T(8,128)}), f32[128,128]{0,1:T(8,128)}) %all-reduce.3.cloned.1.call-update) | async-done | bytes 65552 | tf_op jit(solution)/shard_map/psum | solution.py:48
  327.3 11.7 %cholesky.44 = f32[128,128]{1,0:T(8,128)S(1)} custom-call(f32[128,128]{1,0:T(8,128)S(1)} %fusion.45), custom_call_target="Cholesky" | custom-call | tf_op jit(solution)/shard_map/jit(cholesky)/cholesky | solution.py:49
  340.4 9.8 %custom-call.6 = f32[1,128,128]{1,2,0:T(8,128)S(1)} custom-call(f32[1,128,128]{2,1,0:T(8,128)S(1)} %fusion.40), custom_call_target="InvertDiagBlocksLowerTriangular" | custom-call | tf_op jit(solution)/shard_map/triangular_solve/custom-call.0 | solution.py:51
  350.5 2.3 convolution_convert_fusion
  352.9 1.4 stack.7
  354.3 54.4 %all_to_all.10 = bf16[8,4,256,128]{3,2,1,0:T(8,128)(2,1)} all-to-all(bf16[8,4,256,128]{3,2,1,0:T(8,128)(2,1)S(1)} %stack.7), channel_id=1, replica_groups=mesh['grp'=32,'blk'=8] {'blk'}, dimensions={0} | all-to-all | bytes 4194304 | tf_op jit(solution)/shard_map/all_to_all | solution.py:28
  408.7 4.6 gather_fusion.3
  413.3 5.4 gather_fusion.4
  418.7 2.7 convolution_bitcast_fusion
  421.5 5.2 fusion.21
  428.7 2.0 copy.37
  430.8 231.3 %all-reduce.5.cloned.1.call-done = f32[128,128]{0,1:T(8,128)} async-done(((f32[128,128]{0,1:T(8,128)}), f32[128,128]{0,1:T(8,128)}) %all-reduce.5.cloned.1.call-update) | async-done | bytes 65552 | tf_op jit(solution)/shard_map/psum | solution.py:48
  663.8 11.7 %cholesky.55 = f32[128,128]{1,0:T(8,128)S(1)} custom-call(f32[128,128]{1,0:T(8,128)S(1)} %fusion.43), custom_call_target="Cholesky" | custom-call | tf_op jit(solution)/shard_map/jit(cholesky)/cholesky | solution.py:49
  676.9 9.8 %custom-call.7 = f32[1,128,128]{1,2,0:T(8,128)S(1)} custom-call(f32[1,128,128]{2,1,0:T(8,128)S(1)} %fusion.41), custom_call_target="InvertDiagBlocksLowerTriangular" | custom-call | tf_op jit(solution)/shard_map/triangular_solve/custom-call.0 | solution.py:51
  687.0 2.4 fusion.46
  (58 shorter events, 13.7 us)
Async XLA Ops:
  6.5 71.3 %copy-start = (bf16[24,256,256]{2,1,0:T(8,128)(2,1)S(1)}, bf16[24,256,256]{2,1,0:T(8,128)(2,1)}, u32[]{:S(2)}) copy-start(bf16[24,256,256]{2,1,0:T(8,128)(2,1)} %param.11) | copy-start | bytes 9437188
  6.5 13.3 %copy-start.6 = (s32[1,64]{1,0:T(1,128)S(1)}, s32[1,64]{1,0:T(1,128)}, u32[]{:S(2)}) copy-start(s32[1,64]{1,0:T(1,128)} %param.10) | copy-start | bytes 772
  6.5 13.9 %copy-start.7 = (s32[1,24]{1,0:T(1,128)S(1)}, s32[1,24]{1,0:T(1,128)}, u32[]{:S(2)}) copy-start(s32[1,24]{1,0:T(1,128)} %param.12) | copy-start | bytes 292
  6.5 14.8 %copy-start.1 = (s32[1,32]{1,0:T(1,128)S(1)}, s32[1,32]{1,0:T(1,128)}, u32[]{:S(2)}) copy-start(s32[1,32]{1,0:T(1,128)} %param.13) | copy-start | bytes 388
  6.5 65.9 %all-gather.3.cloned.1.call-start = ((), (), s32[]{:S(2)}) async-start(), calls=%async_computation.2 | async-start | bytes 8650752 | tf_op jit(solution)/shard_map/all_gather | solution.py:35
  10.2 57.5 %all-to-all-start = ((bf16[8,4,256,128]{3,2,1,0:T(8,128)(2,1)}), bf16[8,4,256,128]{3,2,1,0:T(8,128)(2,1)}, u32[]{:S(2)}, u32[]{:S(2)}) async-start(bf16[8,4,256,128]{3,2,1,0:T(8,128)(2,1)} %stack.6), calls=%async_computation | async-start | bytes 4194304 | tf_op jit(solution)/shard_map/all_to_all | solution.py:28
  19.2 306.3 %all-reduce.3.cloned.1.call-start = ((), (), s32[]{:S(2)}) async-start(), calls=%async_computation.3 | async-start | bytes 131072 | tf_op jit(solution)/shard_map/psum | solution.py:48
  77.8 2.7 copy-start.5
  85.8 0.8 copy-start.2
  87.8 325.5 %all-gather.5.cloned.1.call-start = ((), (), s32[]{:S(2)}) async-start(), calls=%async_computation.4 | async-start | bytes 8650752 | tf_op jit(solution)/shard_map/all_gather | solution.py:35
  352.8 309.2 %all-reduce.5.cloned.1.call-start = ((), (), s32[]{:S(2)}) async-start(), calls=%async_computation.5 | async-start | bytes 131072 | tf_op jit(solution)/shard_map/psum | solution.py:48
  418.7 2.7 copy-start.4
  426.7 0.8 copy-start.3
Sparse Core Ops, SparseCore 0:
  9.9 62.1 all-gather.2
  87.9 237.5 all-reduce.2
  353.0 54.4 all-gather.4
  428.8 233.1 all-reduce.4
